TPU v7x, 256 devices: a whole 4x4x8 slice. The times are simulated.
256 devices in a mesh: seq: 16 (over z, x_lo), wr: 4 (over y), wc: 4 (over x_hi, core).
Axes of the slice: x: 4 (x_hi: 2, x_lo: 2; x = x_hi * 2 + x_lo), y: 4, z: 8, core: 2. Of those that a mesh axis runs over, the one named last changes fastest.
Arguments:
- tokens: bfloat16 [8192, 2048], P('seq', ('wr', 'wc')), may hold values from -6 to 6
- ln_gain: float32 [2, 2048], replicated, may hold values from 0.5 to 1.5
- w_branch: bfloat16 [2, 2048, 4096], P(None, None, ('wr', 'wc')), may hold values from -0.125 to 0.125
- w_outgate: bfloat16 [2, 2048, 4096], P(None, None, ('wr', 'wc')), may hold values from -0.125 to 0.125
- w_gates: bfloat16 [2, 2048, 8], replicated, may hold values from -0.125 to 0.125
- forget_bias: float32 [2, 4], replicated, may hold values from 3.2 to 11
- conv_weight: float32 [2, 4, 4096], P(None, None, ('wr', 'wc')), may hold values from -3 to 3
- conv_bias: float32 [2, 4096], P(None, ('wr', 'wc')), may hold values from -3 to 3
- w_query: float32 [2, 4, 4, 4, 256], P(None, 'wr'), may hold values from -3 to 3
- w_key: float32 [2, 4, 4, 4, 256], P(None, 'wr'), may hold values from -3 to 3
- w_value: float32 [2, 4, 4, 4, 256], P(None, 'wr', None, 'wc'), may hold values from -4 to 4
- skip_gain: float32 [2, 4096], P(None, ('wr', 'wc')), may hold values from 0.5 to 1.5
- norm_gain: float32 [2, 4096], P(None, ('wr', 'wc')), may hold values from 0.5 to 1.5
- w_down: bfloat16 [2, 4096, 2048], P(None, ('wr', 'wc')), may hold values from -0.125 to 0.125
- lengths: int32 [3], replicated, may hold values from 1 to 4096, 8192 in all
- request_prompt: int32 [32], P('seq'), may hold values from 0 to 2
Outputs:
- mixed: bfloat16 [8192, 2048], P('seq', ('wr', 'wc'))
- request_state: bfloat16 [2, 32, 4, 1024, 1024], P(None, 'seq', 'wr', None, 'wc')
- request_conv: bfloat16 [2, 32, 3, 4096], P(None, 'seq', None, ('wr', 'wc'))
Inputs may be any that keep to these rules, and one draw needn't show every extreme that they name: `lengths`: the 3 prompts lie end to end in order and fill all 8192 positions; the longest has exactly 4096 positions.
All inputs are finite; a program needn't handle non-finite values.
Results may differ from a plain program's by a relative error of at most 0.035.
Values may be sent and summed in bfloat16 or wider, within the bound.
A program may use at most 128 MiB of HBM per device.

v0:
```python
import jax
import jax.numpy as jnp
from jax import lax
from jax.sharding import PartitionSpec as P

HEADS = 4
CONV = 4
LAYERS = 2
PROMPTS = 3
EPSILON = 1e-05
GATE_CAP = 15.0
ROW_DIMS = (((0,), (0,)), ((), ()))
FEATURE_DIMS = (((1,), (1,)), ((), ()))


def shifted(value, axis, steps):
    count = lax.axis_size(axis)
    first, last = (max(0, -steps), min(count, count - steps))
    return lax.ppermute(value, axis, [(source, source + steps) for source in range(first, last)])


def entering_2(shard, axis, join, neutral):
    place = lax.axis_index(axis)
    gathered = jax.tree.map(
        lambda a, kind: lax.all_gather(a.astype(kind), axis), shard, (jnp.bfloat16, jnp.bfloat16)
    )
    state = jax.tree.map(lambda a, e: jnp.zeros_like(a) + jnp.asarray(e, a.dtype), shard, neutral)

    def one(step, state):
        return join(
            state,
            jax.tree.map(
                lambda a, own: lax.dynamic_index_in_dim(a, step, 0, False).astype(own.dtype),
                gathered,
                shard,
            ),
        )

    return lax.fori_loop(0, place, one, state)


def broadcast(shard, axis, root):
    mine = lax.axis_index(axis) == root
    return lax.psum(jnp.where(mine, shard, jnp.zeros_like(shard)), axis)


def norm_rows(source, gain_row):
    widened = source.astype(jnp.float32)
    row_mean = jnp.mean(widened, axis=1, keepdims=True)
    row_var = jnp.mean(widened * widened, axis=1, keepdims=True) - row_mean * row_mean
    return ((widened - row_mean) * lax.rsqrt(row_var + EPSILON) * gain_row).astype(jnp.bfloat16)


def segment_of(positions, lengths):
    bound_one = lengths[0]
    bound_two = lengths[0] + lengths[1]
    return (positions >= bound_one).astype(jnp.int32) + (positions >= bound_two).astype(jnp.int32)


def conv_rows(extended, ext_segment, segment, weight, bias_row):
    row_count = segment.shape[0]
    widened = extended.astype(jnp.float32)
    summed = jnp.zeros((row_count, widened.shape[1]), jnp.float32) + bias_row
    for back_step in range(weight.shape[0]):
        low_row = weight.shape[0] - 1 - back_step
        keep_row = (ext_segment[low_row : low_row + row_count] == segment).astype(jnp.float32)
        summed = (
            summed + weight[back_step] * widened[low_row : low_row + row_count] * keep_row[:, None]
        )
    return jax.nn.silu(summed).astype(jnp.bfloat16)


def block_mix(source, weight):
    row_count = source.shape[0]
    grouped = source.astype(jnp.float32).reshape(row_count, 4, -1)
    mixed = jnp.einsum("tig,ijg->tjg", grouped, weight, precision=lax.Precision.HIGHEST)
    return mixed.reshape(row_count, -1)


def block_terms(queries, key_rows, values, log_forget, in_gate, segment, prev_seg):
    row_count = queries.shape[0]
    cum_log = jnp.cumsum(log_forget)
    row_order = jnp.arange(row_count)
    allowed = (row_order[:, None] >= row_order[None, :]) & (segment[:, None] == segment[None, :])
    exponent = jnp.where(allowed, cum_log[:, None] - cum_log[None, :] + in_gate[None, :], -jnp.inf)
    scores = lax.dot_general(
        queries, key_rows, FEATURE_DIMS, preferred_element_type=jnp.float32
    ) * jnp.exp(exponent)
    in_block = jnp.dot(scores.astype(jnp.bfloat16), values, preferred_element_type=jnp.float32)
    carried = jnp.where(segment == prev_seg, jnp.exp(cum_log), 0.0)
    last_seg = segment[row_count - 1]
    weights = jnp.where(
        segment == last_seg, jnp.exp(cum_log[row_count - 1] - cum_log + in_gate), 0.0
    )
    weighted = (key_rows.astype(jnp.float32) * weights[:, None]).astype(jnp.bfloat16)
    increment = lax.dot_general(weighted, values, ROW_DIMS, preferred_element_type=jnp.float32)
    block_decay = jnp.where(last_seg == prev_seg, jnp.exp(cum_log[row_count - 1]), 0.0)
    return (in_block, carried, increment, block_decay)


def end_state(
    state_in, key_rows, values, cum_log, in_gate, segment, seg_before, local_end, prompt, holder
):
    end_cum = cum_log[local_end]
    entering = jnp.where(holder & (seg_before == prompt), jnp.exp(end_cum), 0.0)
    row_order = jnp.arange(segment.shape[0])
    chosen = holder & (segment == prompt) & (row_order <= local_end)
    weights = jnp.where(chosen, jnp.exp(end_cum - cum_log + in_gate), 0.0)
    weighted = (key_rows.astype(jnp.float32) * weights[:, None]).astype(jnp.bfloat16)
    return entering * state_in + lax.dot_general(
        weighted, values, ROW_DIMS, preferred_element_type=jnp.float32
    )


def combine_states(earlier, later):
    return (earlier[0] * later[0], later[0] * earlier[1] + later[1])


def body(
    tokens,
    ln_gain,
    w_branch,
    w_outgate,
    w_gates,
    forget_bias,
    conv_weight,
    conv_bias,
    w_query,
    w_key,
    w_value,
    skip_gain,
    norm_gain,
    w_down,
    lengths,
    request_prompt,
):
    tok_rows = tokens.shape[0]
    seq_count = lax.axis_size("seq")
    seq_index = lax.axis_index("seq")
    head_idx = lax.axis_index("wr")
    row_offset = seq_index * tok_rows
    total_rows = tok_rows * seq_count
    row_ids = jnp.arange(tok_rows, dtype=jnp.int32)
    positions = row_offset + row_ids
    segment = segment_of(positions, lengths)
    seg_before = jnp.where(row_offset > 0, segment_of(row_offset - 1, lengths), -1)
    rim_positions = row_offset - (CONV - 1) + jnp.arange(CONV - 1, dtype=jnp.int32)
    rim_segment = jnp.where(rim_positions >= 0, segment_of(rim_positions, lengths), -1)
    ext_segment = jnp.concatenate([rim_segment, segment])
    prompt_starts = [jnp.zeros((), jnp.int32), lengths[0], lengths[0] + lengths[1]]
    prompt_ends = [
        lengths[0] - 1,
        lengths[0] + lengths[1] - 1,
        jnp.zeros((), jnp.int32) + (total_rows - 1),
    ]
    head_mask = (jnp.arange(HEADS, dtype=jnp.int32) == head_idx).astype(jnp.float32)
    current = tokens
    sent_states = []
    sent_edges = []
    for layer_idx in range(LAYERS):
        gathered = lax.all_gather(current, ("wr", "wc"), axis=1, tiled=True)
        normed = norm_rows(gathered, ln_gain[layer_idx])
        branch = jnp.dot(normed, w_branch[layer_idx], preferred_element_type=jnp.float32).astype(
            jnp.bfloat16
        )
        outgate = jnp.dot(normed, w_outgate[layer_idx], preferred_element_type=jnp.float32)
        gate_pre = jnp.dot(normed, w_gates[layer_idx], preferred_element_type=jnp.float32)
        input_pre = jnp.sum(gate_pre[:, :HEADS] * head_mask, axis=1)
        forget_pre = jnp.sum((gate_pre[:, HEADS:] + forget_bias[layer_idx]) * head_mask, axis=1)
        in_gate = GATE_CAP * jnp.tanh(input_pre / GATE_CAP)
        log_forget = jax.nn.log_sigmoid(forget_pre)
        edge_in = shifted(branch[tok_rows - (CONV - 1) :], "seq", 1)
        extended = jnp.concatenate([edge_in, branch], axis=0)
        conv_act = conv_rows(
            extended, ext_segment, segment, conv_weight[layer_idx], conv_bias[layer_idx]
        )
        head_branch, head_act = (
            lax.all_gather(branch, "wc", axis=1, tiled=True),
            lax.all_gather(conv_act, "wc", axis=1, tiled=True),
        )
        head_width = head_act.shape[1]
        queries = block_mix(head_act, w_query[layer_idx, 0]).astype(jnp.bfloat16)
        key_rows = (block_mix(head_act, w_key[layer_idx, 0]) * head_width ** (-0.5)).astype(
            jnp.bfloat16
        )
        values = block_mix(head_branch, w_value[layer_idx, 0]).astype(jnp.bfloat16)
        prefix = jnp.zeros((head_width, values.shape[1]), jnp.float32)
        reach_all = jnp.ones((), jnp.float32)
        in_block, carried, increment, block_decay = block_terms(
            queries, key_rows, values, log_forget, in_gate, segment, seg_before
        )
        saved_parts = (in_block, carried, reach_all, prefix)
        prefix = block_decay * prefix + increment
        reach_all = block_decay * reach_all
        entering = entering_2(
            (reach_all, prefix),
            "seq",
            combine_states,
            (jnp.ones((), jnp.float32), jnp.zeros_like(prefix)),
        )[1]
        in_block, carried, reach_here, prefix_here = saved_parts
        state_here = (reach_here * entering + prefix_here).astype(jnp.bfloat16)
        hidden_parts = in_block + carried[:, None] * jnp.dot(
            queries, state_here, preferred_element_type=jnp.float32
        )
        sums_one, sums_two = lax.psum(
            (jnp.sum(hidden_parts, axis=1), jnp.sum(hidden_parts * hidden_parts, axis=1)), "wc"
        )
        row_mean = sums_one / head_width
        row_var = sums_two / head_width - row_mean * row_mean
        normal_rows = (hidden_parts - row_mean[:, None]) * lax.rsqrt(row_var + EPSILON)[:, None]
        gated = (
            (
                normal_rows * norm_gain[layer_idx]
                + skip_gain[layer_idx] * conv_act.astype(jnp.float32)
            )
            * jax.nn.silu(outgate)
        ).astype(jnp.bfloat16)
        term_rows = jnp.dot(gated, w_down[layer_idx], preferred_element_type=jnp.float32)
        summed = lax.psum_scatter(
            term_rows.astype(jnp.bfloat16), ("wr", "wc"), scatter_dimension=1, tiled=True
        ).astype(jnp.float32)
        current = (current.astype(jnp.float32) + summed).astype(jnp.bfloat16)
        cum_log = jnp.cumsum(log_forget)
        for prompt in range(PROMPTS):
            end_pos = prompt_ends[prompt]
            holder = (end_pos >= row_offset) & (end_pos < row_offset + tok_rows)
            local_end = jnp.clip(end_pos - row_offset, 0, tok_rows - 1)
            state_end = end_state(
                entering,
                key_rows,
                values,
                cum_log,
                in_gate,
                segment,
                seg_before,
                local_end,
                prompt,
                holder,
            )
            window = lax.dynamic_slice_in_dim(extended, local_end + 1, CONV - 1, 0)
            edge_pos = end_pos - (CONV - 2) + jnp.arange(CONV - 1, dtype=jnp.int32)
            edge_rows = jnp.where(
                ((edge_pos >= prompt_starts[prompt]) & holder)[:, None],
                window,
                jnp.zeros_like(window),
            )
            got_state, got_edge = (
                broadcast(state_end.astype(jnp.bfloat16), "seq", end_pos // tok_rows),
                broadcast(edge_rows, "seq", end_pos // tok_rows),
            )
            sent_states.append(got_state)
            sent_edges.append(got_edge)
    state_stack = jnp.stack(sent_states)
    edge_stack = jnp.stack(sent_edges)
    state_stack = state_stack.reshape(LAYERS, PROMPTS, state_stack.shape[1], state_stack.shape[2])
    edge_stack = edge_stack.reshape(LAYERS, PROMPTS, edge_stack.shape[1], edge_stack.shape[2])
    chooser = (request_prompt[:, None] == jnp.arange(PROMPTS, dtype=jnp.int32)[None, :]).astype(
        jnp.bfloat16
    )
    request_state = jnp.einsum(
        "rp,lphd->lrhd", chooser, state_stack, preferred_element_type=jnp.float32
    ).astype(jnp.bfloat16)[:, :, None]
    request_conv = jnp.einsum(
        "rp,lpkc->lrkc", chooser, edge_stack, preferred_element_type=jnp.float32
    ).astype(jnp.bfloat16)
    return (current, request_state, request_conv)


def solution(mesh):
    return jax.shard_map(
        body,
        mesh=mesh,
        in_specs=(
            P("seq", ("wr", "wc")),
            P(),
            P(None, None, ("wr", "wc")),
            P(None, None, ("wr", "wc")),
            P(),
            P(),
            P(None, None, ("wr", "wc")),
            P(None, ("wr", "wc")),
            P(None, "wr", None, None, None),
            P(None, "wr", None, None, None),
            P(None, "wr", None, "wc", None),
            P(None, ("wr", "wc")),
            P(None, ("wr", "wc")),
            P(None, ("wr", "wc"), None),
            P(),
            P("seq"),
        ),
        out_specs=(
            P("seq", ("wr", "wc")),
            P(None, "seq", "wr", None, "wc"),
            P(None, "seq", None, ("wr", "wc")),
        ),
        check_vma=False,
    )
```

profile of v0, /device:TPU:8, one launch (start us, length us, event | category | flops | bytes accessed | tf_op | source)
XLA Modules:
  0.0 1085.9 jit_solution(4009449505985787538)
XLA Ops:
  17.0 47.1 %all-gather.11.cloned.1.call-done = bf16[512,2048]{1,0:T(8,128)(2,1)} async-done(((bf16[512,128]{1,0:T(8,128)(2,1)}), bf16[512,2048]{1,0:T(8,128)(2,1)}) %all-gather.11.cloned.1.call-update) | async-done | bytes 2097168 | tf_op jit(solution)/shard_map/all_gather | solution.py:161
  64.1 2.4 convert_reduce_fusion.1
  71.5 2.5 collective-permute-start
  83.8 8.9 all-gather.15.cloned.1.call-done
  97.7 19.7 %all-gather.13.cloned.1.call-done = bf16[512,1024]{1,0:T(8,128)(2,1)} async-done(((bf16[512,256]{1,0:T(8,128)(2,1)}), bf16[512,1024]{1,0:T(8,128)(2,1)}) %all-gather.13.cloned.1.call-update) | async-done | bytes 1048592 | tf_op jit(solution)/shard_map/all_gather | solution.py:179
  117.4 2.6 reshape.474
  120.0 2.8 copy.89
  122.8 4.2 fusion.99
  127.0 2.9 copy.92
  129.9 3.2 fusion.16
  133.2 2.4 copy.95
  135.5 2.5 fusion.30
  144.2 38.1 %all-reduce = bf16[16]{0:T(256)(128)(2,1)S(1)} all-reduce(bf16[16]{0:T(256)(128)(2,1)} %dynamic-update-slice), channel_id=1, replica_groups=mesh['seq'=16,'wr'=4,'wc'=4] {'seq'}, use_global_device_ids=true, to_apply=%add | all-reduce | flops 16 | bytes 64
  182.3 2.9 fusion.26
  187.8 3.2 fusion.53
  191.0 130.3 %all-gather.23.cloned.1.call-done = bf16[16384,256]{1,0:T(8,128)(2,1)} async-done(((bf16[1024,256]{1,0:T(8,128)(2,1)}), bf16[16384,256]{1,0:T(8,128)(2,1)}) %all-gather.23.cloned.1.call-update) | async-done | bytes 8388624 | tf_op jit(solution)/shard_map/all_gather | solution.py:25
  322.1 2.7 fusion.217
  324.8 9.4 all-reduce.3
  334.9 5.5 convolution_convert_fusion.1
  340.4 3.9 copy.136
  344.4 114.9 %reduce-scatter.7.cloned.1.call-done = bf16[128,512]{1,0:T(8,128)(2,1)} async-done(((bf16[2048,512]{1,0:T(8,128)(2,1)}), bf16[128,512]{1,0:T(8,128)(2,1)}) %reduce-scatter.7.cloned.1.call-update) | async-done | bytes 131088
  461.1 51.2 %all-gather.17.cloned.1.call-done = bf16[512,2048]{1,0:T(8,128)(2,1)} async-done(((bf16[512,128]{1,0:T(8,128)(2,1)}), bf16[512,2048]{1,0:T(8,128)(2,1)}) %all-gather.17.cloned.1.call-update) | async-done | bytes 2097168 | tf_op jit(solution)/shard_map/all_gather | solution.py:161
  512.3 2.4 convert_reduce_fusion
  518.6 2.5 collective-permute-start.1
  529.3 3.2 exponential_select_fusion.1
  532.5 8.4 all-gather.21.cloned.1.call-done
  545.0 20.6 %all-gather.19.cloned.1.call-done = bf16[512,1024]{1,0:T(8,128)(2,1)} async-done(((bf16[512,256]{1,0:T(8,128)(2,1)}), bf16[512,1024]{1,0:T(8,128)(2,1)}) %all-gather.19.cloned.1.call-update) | async-done | bytes 1048592 | tf_op jit(solution)/shard_map/all_gather | solution.py:179
  568.9 4.2 fusion.96
  573.1 2.9 copy.102
  576.0 2.8 fusion.23
  580.7 2.3 copy.105
  583.0 2.5 fusion.31
  590.7 71.5 %all-reduce.4 = (bf16[16]{0:T(256)(128)(2,1)S(1)}, bf16[1,3,256]{2,1,0:T(4,128)(2,1)S(1)}, bf16[1,3,256]{2,1,0:T(4,128)(2,1)S(1)}, bf16[1,3,256]{2,1,0:T(4,128)(...) all-reduce(bf16[16]{0:T(256)(128)(2,1)S(1)} %dynamic-update-slice.1, ...), channel_id=1, replica_groups=mesh['seq'=16,'wr'=4,'wc'=4] {'seq'}, use_global_device_ids=true, to_apply=%add.1 | all-reduce | flops 4624 | bytes 18496
  662.2 2.9 fusion.27
  667.5 3.3 fusion.52
  670.8 99.3 %all-gather.25.cloned.1.call-done = bf16[16384,256]{1,0:T(8,128)(2,1)} async-done(((bf16[1024,256]{1,0:T(8,128)(2,1)}), bf16[16384,256]{1,0:T(8,128)(2,1)}) %all-gather.25.cloned.1.call-update) | async-done | bytes 8388624 | tf_op jit(solution)/shard_map/all_gather | solution.py:25
  770.5 2.7 fusion.216
  773.1 8.8 all-reduce.2
  782.0 6.1 convolution_convert_fusion
  788.1 3.9 copy.138
  798.1 3.4 fusion.19
  803.8 2.3 copy.109
  806.0 2.3 copy.108
  808.3 2.6 fusion.47
  813.5 2.4 copy.113
  823.8 82.0 %reduce-scatter.9.cloned.1.call-done = bf16[128,512]{1,0:T(8,128)(2,1)} async-done(((bf16[2048,512]{1,0:T(8,128)(2,1)}), bf16[128,512]{1,0:T(8,128)(2,1)}) %reduce-scatter.9.cloned.1.call-update) | async-done | bytes 131088
  907.5 164.3 %all-reduce.8.cloned.1.call-done = (bf16[1,1024,256]{2,1,0:T(8,128)(2,1)}, bf16[1,1024,256]{2,1,0:T(8,128)(2,1)}, bf16[1,1024,256]{2,1,0:T(8,128)(2,1)}, bf16[1,...) async-done(((bf16[1,1024,256]{2,1,0:T(8,128)(2,1)}, bf16[1,1024,256]{2,1,0:T(8,128)(2,1)}, bf16[1,1024,256]{2,1,0:T(8,128)(2,1)}, ...) | async-done | bytes 3145744 | tf_op jit(solution)/shard_map/psum | solution.py:44
  1074.4 3.1 fusion.13
  (230 shorter events, 85.2 us)
Async XLA Ops:
  7.2 56.9 %all-gather.11.cloned.1.call-start = ((), (), s32[]{:S(2)}) async-start(), calls=%async_computation.2 | async-start | bytes 2228224 | tf_op jit(solution)/shard_map/all_gather | solution.py:161
  7.9 84.8 %all-gather.15.cloned.1.call-start = ((), (), s32[]{:S(2)}) async-start(), calls=%async_computation.4 | async-start | bytes 1310720 | tf_op jit(solution)/shard_map/all_gather | solution.py:178
  11.3 59.7 %copy-start.39 = (f32[4]{0:T(128)}, f32[4]{0:T(128)S(1)}, u32[]{:S(2)}) copy-start(f32[4]{0:T(128)S(1)} %compare_convert_fusion) | copy-start | bytes 52
  64.1 2.5 copy-start.1
  68.1 2.2 copy-start.22
  69.6 6.1 copy-start.15
  69.6 47.8 %all-gather.13.cloned.1.call-start = ((), (), s32[]{:S(2)}) async-start(), calls=%async_computation.3 | async-start | bytes 1310720 | tf_op jit(solution)/shard_map/all_gather | solution.py:179
  71.0 6.7 copy-start.29
  71.0 7.3 copy-start.23
  71.1 10.8 copy-start.24
  71.5 4.1 collective-permute-start
  75.5 8.3 copy-start.30
  75.7 8.1 copy-start.27
  76.9 244.4 %all-gather.23.cloned.1.call-start = ((), (), s32[]{:S(2)}) async-start(), calls=%async_computation.8 | async-start | bytes 8912896 | tf_op jit(solution)/shard_map/all_gather | solution.py:25
  133.1 4.9 copy-start.49
  133.1 5.5 copy-start.41
  133.2 6.1 copy-start.42
  138.0 321.3 %reduce-scatter.7.cloned.1.call-start = ((), (), s32[]{:S(2)}) async-start(), calls=%async_computation.10 | async-start | bytes 2228224
  182.3 5.1 copy-start.31
  182.3 5.1 copy-start.38
  344.3 116.0 %copy-start.17 = (bf16[512,128]{1,0:T(8,128)(2,1)S(1)}, bf16[512,128]{1,0:T(8,128)(2,1)}, u32[]{:S(2)}) copy-start(bf16[512,128]{1,0:T(8,128)(2,1)} %param.20) | copy-start | bytes 393220
  344.3 168.0 %all-gather.17.cloned.1.call-start = ((), (), s32[]{:S(2)}) async-start(), calls=%async_computation.5 | async-start | bytes 2228224 | tf_op jit(solution)/shard_map/all_gather | solution.py:161
  461.0 79.9 %all-gather.21.cloned.1.call-start = ((), (), s32[]{:S(2)}) async-start(), calls=%async_computation.7 | async-start | bytes 1310720 | tf_op jit(solution)/shard_map/all_gather | solution.py:178
  512.3 2.5 copy-start.2
  516.4 10.1 copy-start
  516.4 7.0 copy-start.34
  516.4 7.0 copy-start.35
  516.4 7.0 copy-start.36
  516.4 7.0 copy-start.37
  517.8 7.6 copy-start.26
  517.8 47.8 %all-gather.19.cloned.1.call-start = ((), (), s32[]{:S(2)}) async-start(), calls=%async_computation.6 | async-start | bytes 1310720 | tf_op jit(solution)/shard_map/all_gather | solution.py:179
  518.6 3.8 collective-permute-start.1
  525.2 2.0 copy-start.43
  525.2 244.9 %all-gather.25.cloned.1.call-start = ((), (), s32[]{:S(2)}) async-start(), calls=%async_computation.9 | async-start | bytes 8912896 | tf_op jit(solution)/shard_map/all_gather | solution.py:25
  583.0 5.1 copy-start.28
  585.6 320.2 %reduce-scatter.9.cloned.1.call-start = ((), (), s32[]{:S(2)}) async-start(), calls=%async_computation.11 | async-start | bytes 2228224
  662.2 5.1 copy-start.32
  770.4 11.5 %copy-start.44 = (f32[1,256]{1,0:T(1,128)S(1)}, f32[1,256]{1,0:T(1,128)}, u32[]{:S(2)}) copy-start(f32[1,256]{1,0:T(1,128)} %get-tuple-element.222) | copy-start | bytes 3076
  770.4 11.5 %copy-start.45 = (f32[1,256]{1,0:T(1,128)S(1)}, f32[1,256]{1,0:T(1,128)}, u32[]{:S(2)}) copy-start(f32[1,256]{1,0:T(1,128)} %get-tuple-element.220) | copy-start | bytes 3076
  792.0 4.2 copy-start.25
  792.0 279.8 %all-reduce.8.cloned.1.call-start = ((), (), s32[]{:S(2)}) async-start(), calls=%async_computation.12 | async-start | bytes 6291456 | tf_op jit(solution)/shard_map/psum | solution.py:44
  808.3 2.6 copy-start.8
  813.5 2.4 copy-start.3
  815.9 2.7 copy-start.14
  822.3 84.5 %copy-start.16 = (bf16[512,128]{1,0:T(8,128)(2,1)S(1)}, bf16[512,128]{1,0:T(8,128)(2,1)}, u32[]{:S(2)}) copy-start(bf16[512,128]{1,0:T(8,128)(2,1)} %add_convert_fusion.1) | copy-start | bytes 393220
  1071.8 2.4 copy-start.21
  1071.9 2.4 copy-start.20
  1071.9 2.5 copy-start.19
  (15 other events, 19.8 us)
Sparse Core Ops, SparseCore 0:
  10.6 53.4 all-gather.10
  69.7 22.9 all-gather.14
  94.5 22.8 all-gather.12
  138.1 183.1 all-gather.22
  344.4 114.8 reduce-scatter.6
  462.3 49.9 all-gather.16
  518.0 22.8 all-gather.20
  542.7 22.8 all-gather.18
  585.7 184.3 all-gather.24
  792.1 113.6 reduce-scatter.8
  908.9 162.8 all-reduce.7
where the time goes:
time: 1100 us; the launch traced here: 1090 us
  waiting for transfers between devices  749 us (68%)
  blocking collectives  128 us (12%)
  local copies, waits for them, and re-layouts  79.5 us (7%)
  matrix products  59.7 us (5%)
  other arithmetic  39.7 us (4%)
  between operations  24.4 us (2%)
    all_gather x2, waiting for transfers between devices, entering_2(): lax.all_gather(a.astype(kind), axis)  230 us
    unnamed x13, waiting for transfers between devices  198 us
    psum x1, waiting for transfers between devices, broadcast(): return lax.psum(jnp.where(mine, shard, jnp.zeros_like(shard)), axis)  164 us
    unnamed x2, blocking collectives  110 us
    all_gather x2, waiting for transfers between devices, body(): gathered = lax.all_gather(current, ('wr', 'wc'), axis=1, tiled=True)  98.3 us
    all_gather x2, waiting for transfers between devices, body(): lax.all_gather(conv_act, 'wc', axis=1, tiled=True)  40.3 us
    unnamed x126, local copies, waits for them, and re-layouts  27.7 us
  transfers between devices with their start and end apart: 13, of which 12 were waited for; matrix products, arithmetic and copies ran while one was open for 8% of the time, Pallas kernels for 0%

commit v1 on v0

--- a/solution.py
+++ b/solution.py
@@ -41,7 +41,7 @@
 
 def broadcast(shard, axis, root):
     mine = lax.axis_index(axis) == root
-    return lax.psum(jnp.where(mine, shard, jnp.zeros_like(shard)), axis)
+    return jnp.sum(lax.all_gather(jnp.where(mine, shard, jnp.zeros_like(shard)), axis), axis=0)
 
 
 def norm_rows(source, gain_row):

time: 1100 us -> 2000 us (1.82)
  waiting for transfers between devices: 749 us -> 1420 us
  blocking collectives: 128 us -> 328 us
  other arithmetic: 39.7 us -> 66.7 us
    all_gather x0 -> x6, waiting for transfers between devices: none -> 825 us  [broadcast(): lax.all_gather(jnp.where(mine, shard, jnp.zeros_like(shard)), axis)]
    all_gather x0 -> x6, blocking collectives: none -> 236 us  [broadcast(): lax.all_gather(jnp.where(mine, shard, jnp.zeros_like(shard)), axis)]
    psum x1 -> x0, waiting for transfers between devices: 164 us -> none  [broadcast(): return lax.psum(jnp.where(mine, shard, jnp.zeros_like(shard)), axis)]
    unnamed x2, blocking collectives: 110 us -> 73.9 us
    reduce_sum x0 -> x12, other arithmetic: none -> 29.2 us  [broadcast(): jnp.sum(lax.all_gather(jnp.where(mine, shard, jnp.zeros_like(shard)), axi...]
    unnamed x13 -> x18, waiting for transfers between devices: 198 us -> 192 us
  transfers between devices with their start and end apart: 13 -> 18, of which waited for: 12 -> 16; matrix products, arithmetic and copies ran while one was open for 8% -> 6% of each run, Pallas kernels for 0% -> 0%
where the time goes in v1:
time: 2000 us; the launch traced here: 1990 us
  waiting for transfers between devices  1420 us (71%)
  blocking collectives  328 us (16%)
  local copies, waits for them, and re-layouts  75 us (4%)
  other arithmetic  66.7 us (3%)
  matrix products  62 us (3%)
  between operations  24.5 us (1%)
    all_gather x6, waiting for transfers between devices, broadcast(): lax.all_gather(jnp.where(mine, shard, jnp.zeros_like(shard)), axis)  825 us
    all_gather x2, waiting for transfers between devices, entering_2(): lax.all_gather(a.astype(kind), axis)  249 us
    all_gather x6, blocking collectives, broadcast(): lax.all_gather(jnp.where(mine, shard, jnp.zeros_like(shard)), axis)  236 us
    unnamed x18, waiting for transfers between devices  192 us
    all_gather x2, waiting for transfers between devices, body(): gathered = lax.all_gather(current, ('wr', 'wc'), axis=1, tiled=True)  98.4 us
    unnamed x2, blocking collectives  73.9 us
    all_gather x2, waiting for transfers between devices, body(): lax.all_gather(conv_act, 'wc', axis=1, tiled=True)  40.3 us
  transfers between devices with their start and end apart: 18, of which 16 were waited for; matrix products, arithmetic and copies ran while one was open for 6% of the time, Pallas kernels for 0%

profile of v1, /device:TPU:8, one launch (start us, length us, event | category | flops | bytes accessed | tf_op | source)
XLA Modules:
  0.0 1985.9 jit_solution(12658136994103058370)
XLA Ops:
  16.9 47.1 %all-gather.35.cloned.1.call-done = bf16[512,2048]{1,0:T(8,128)(2,1)} async-done(((bf16[512,128]{1,0:T(8,128)(2,1)}), bf16[512,2048]{1,0:T(8,128)(2,1)}) %all-gather.35.cloned.1.call-update) | async-done | bytes 2097168 | tf_op jit(solution)/shard_map/all_gather | solution.py:161
  83.7 8.9 all-gather.39.cloned.1.call-done
  97.7 19.7 all-gather.37.cloned.1.call-done
  122.8 4.2 fusion.93
  127.1 2.9 copy.90
  130.0 3.2 fusion.16
  144.0 38.8 %all-reduce = bf16[16]{0:T(256)(128)(2,1)S(1)} all-reduce(bf16[16]{0:T(256)(128)(2,1)} %dynamic-update-slice), channel_id=1, replica_groups=mesh['seq'=16,'wr'=4,'wc'=4] {'seq'}, use_global_device_ids=true, to_apply=%add | all-reduce | flops 16 | bytes 64
  182.9 2.9 fusion.26
  188.3 3.2 fusion.47
  191.5 129.7 %all-gather.47.cloned.1.call-done = bf16[16384,256]{1,0:T(8,128)(2,1)} async-done(((bf16[1024,256]{1,0:T(8,128)(2,1)}), bf16[16384,256]{1,0:T(8,128)(2,1)}) %all-gather.47.cloned.1.call-update) | async-done | bytes 8388624 | tf_op jit(solution)/shard_map/all_gather | solution.py:25
  324.7 9.4 all-reduce.3
  334.8 5.5 convolution_convert_fusion.1
  340.3 3.9 copy.134
  344.3 115.0 %reduce-scatter.7.cloned.1.call-done = bf16[128,512]{1,0:T(8,128)(2,1)} async-done(((bf16[2048,512]{1,0:T(8,128)(2,1)}), bf16[128,512]{1,0:T(8,128)(2,1)}) %reduce-scatter.7.cloned.1.call-update) | async-done | bytes 131088
  461.1 51.2 %all-gather.41.cloned.1.call-done = bf16[512,2048]{1,0:T(8,128)(2,1)} async-done(((bf16[512,128]{1,0:T(8,128)(2,1)}), bf16[512,2048]{1,0:T(8,128)(2,1)}) %all-gather.41.cloned.1.call-update) | async-done | bytes 2097168 | tf_op jit(solution)/shard_map/all_gather | solution.py:161
  529.3 3.2 exponential_select_fusion.1
  532.4 8.5 all-gather.45.cloned.1.call-done
  545.1 20.6 %all-gather.43.cloned.1.call-done = bf16[512,1024]{1,0:T(8,128)(2,1)} async-done(((bf16[512,256]{1,0:T(8,128)(2,1)}), bf16[512,1024]{1,0:T(8,128)(2,1)}) %all-gather.43.cloned.1.call-update) | async-done | bytes 1048592 | tf_op jit(solution)/shard_map/all_gather | solution.py:179
  568.9 4.2 fusion.90
  573.1 2.9 copy.100
  576.0 2.8 fusion.23
  587.1 3.0 fusion.19
  606.9 35.1 %all-reduce.1 = bf16[16]{0:T(256)(128)(2,1)S(1)} all-reduce(bf16[16]{0:T(256)(128)(2,1)S(1)} %dynamic-update-slice.1), channel_id=1, replica_groups=mesh['seq'=16,'wr'=4,'wc'=4] {'seq'}, use_global_device_ids=true, to_apply=%add.1 | all-reduce | flops 16 | bytes 64
  642.0 3.0 fusion.27
  648.2 119.6 %all-gather.49.cloned.1.call-done = bf16[16384,256]{1,0:T(8,128)(2,1)} async-done(((bf16[1024,256]{1,0:T(8,128)(2,1)}), bf16[16384,256]{1,0:T(8,128)(2,1)}) %all-gather.49.cloned.1.call-update) | async-done | bytes 8388624 | tf_op jit(solution)/shard_map/all_gather | solution.py:25
  768.0 2.8 fusion.210
  770.8 9.0 all-reduce.2
  779.8 5.5 convolution_convert_fusion
  785.2 3.9 copy.136
  799.0 74.7 %all-gather.16 = bf16[16,3,256]{2,1,0:T(4,128)(2,1)S(1)} all-gather(bf16[1,3,256]{2,1,0:T(4,128)(2,1)S(1)} %get-tuple-element.166), channel_id=12, replica_groups=mesh['seq'=16,'wr'=4,'wc'=4] {'seq'}, dimensions={0}, use_global_device_ids=true | all-gather | bytes 26112 | tf_op jit(solution)/shard_map/all_gather | solution.py:44
  873.7 30.4 %all-gather.14 = bf16[16,3,256]{2,1,0:T(4,128)(2,1)S(1)} all-gather(bf16[1,3,256]{2,1,0:T(4,128)(2,1)S(1)} %get-tuple-element.167), channel_id=10, replica_groups=mesh['seq'=16,'wr'=4,'wc'=4] {'seq'}, dimensions={0}, use_global_device_ids=true | all-gather | bytes 26112 | tf_op jit(solution)/shard_map/all_gather | solution.py:44
  904.2 34.5 %all-gather.15 = bf16[16,3,256]{2,1,0:T(4,128)(2,1)S(1)} all-gather(bf16[1,3,256]{2,1,0:T(4,128)(2,1)S(1)} %get-tuple-element.168), channel_id=11, replica_groups=mesh['seq'=16,'wr'=4,'wc'=4] {'seq'}, dimensions={0}, use_global_device_ids=true | all-gather | bytes 26112 | tf_op jit(solution)/shard_map/all_gather | solution.py:44
  938.9 30.0 %all-gather.19 = bf16[16,3,256]{2,1,0:T(4,128)(2,1)S(1)} all-gather(bf16[1,3,256]{2,1,0:T(4,128)(2,1)S(1)} %get-tuple-element.163), channel_id=15, replica_groups=mesh['seq'=16,'wr'=4,'wc'=4] {'seq'}, dimensions={0}, use_global_device_ids=true | all-gather | bytes 26112 | tf_op jit(solution)/shard_map/all_gather | solution.py:44
  968.9 36.1 %all-gather.17 = bf16[16,3,256]{2,1,0:T(4,128)(2,1)S(1)} all-gather(bf16[1,3,256]{2,1,0:T(4,128)(2,1)S(1)} %get-tuple-element.164), channel_id=13, replica_groups=mesh['seq'=16,'wr'=4,'wc'=4] {'seq'}, dimensions={0}, use_global_device_ids=true | all-gather | bytes 26112 | tf_op jit(solution)/shard_map/all_gather | solution.py:44
  1005.0 30.4 %all-gather.18 = bf16[16,3,256]{2,1,0:T(4,128)(2,1)S(1)} all-gather(bf16[1,3,256]{2,1,0:T(4,128)(2,1)S(1)} %get-tuple-element.165), channel_id=14, replica_groups=mesh['seq'=16,'wr'=4,'wc'=4] {'seq'}, dimensions={0}, use_global_device_ids=true | all-gather | bytes 26112 | tf_op jit(solution)/shard_map/all_gather | solution.py:44
  1036.3 4.8 reduce_sum.266
  1041.1 101.3 %all-gather.53.cloned.1.call-done = bf16[16384,256]{1,0:T(8,128)(2,1)} async-done(((bf16[1024,256]{1,0:T(8,128)(2,1)}), bf16[16384,256]{1,0:T(8,128)(2,1)}) %all-gather.53.cloned.1.call-update) | async-done | bytes 8388624 | tf_op jit(solution)/shard_map/all_gather | solution.py:44
  1142.5 4.8 reduce_sum.265
  1147.3 180.6 %all-gather.51.cloned.1.call-done = bf16[16384,256]{1,0:T(8,128)(2,1)} async-done(((bf16[1024,256]{1,0:T(8,128)(2,1)}), bf16[16384,256]{1,0:T(8,128)(2,1)}) %all-gather.51.cloned.1.call-update) | async-done | bytes 8388624 | tf_op jit(solution)/shard_map/all_gather | solution.py:44
  1327.9 4.8 reduce_sum.264
  1335.3 76.1 %reduce-scatter.9.cloned.1.call-done = bf16[128,512]{1,0:T(8,128)(2,1)} async-done(((bf16[2048,512]{1,0:T(8,128)(2,1)}), bf16[128,512]{1,0:T(8,128)(2,1)}) %reduce-scatter.9.cloned.1.call-update) | async-done | bytes 131088
  1413.1 181.7 %all-gather.61.cloned.1.call-done = bf16[16384,256]{1,0:T(8,128)(2,1)} async-done(((bf16[1024,256]{1,0:T(8,128)(2,1)}), bf16[16384,256]{1,0:T(8,128)(2,1)}) %all-gather.61.cloned.1.call-update) | async-done | bytes 8388624 | tf_op jit(solution)/shard_map/all_gather | solution.py:44
  1594.9 4.8 reduce_sum.269
  1599.7 180.7 %all-gather.57.cloned.1.call-done = bf16[16384,256]{1,0:T(8,128)(2,1)} async-done(((bf16[1024,256]{1,0:T(8,128)(2,1)}), bf16[16384,256]{1,0:T(8,128)(2,1)}) %all-gather.57.cloned.1.call-update) | async-done | bytes 8388624 | tf_op jit(solution)/shard_map/all_gather | solution.py:44
  1780.4 4.8 reduce_sum.267
  1785.2 180.2 %all-gather.59.cloned.1.call-done = bf16[16384,256]{1,0:T(8,128)(2,1)} async-done(((bf16[1024,256]{1,0:T(8,128)(2,1)}), bf16[16384,256]{1,0:T(8,128)(2,1)}) %all-gather.59.cloned.1.call-update) | async-done | bytes 8388624 | tf_op jit(solution)/shard_map/all_gather | solution.py:44
  1965.4 4.8 reduce_sum.268
  1972.8 4.8 fusion.13
  (253 shorter events, 120.8 us)
Async XLA Ops:
  7.2 56.9 %all-gather.35.cloned.1.call-start = ((), (), s32[]{:S(2)}) async-start(), calls=%async_computation.2 | async-start | bytes 2228224 | tf_op jit(solution)/shard_map/all_gather | solution.py:161
  7.9 84.8 %all-gather.39.cloned.1.call-start = ((), (), s32[]{:S(2)}) async-start(), calls=%async_computation.4 | async-start | bytes 1310720 | tf_op jit(solution)/shard_map/all_gather | solution.py:178
  11.3 59.7 %copy-start.34 = (f32[4]{0:T(128)}, f32[4]{0:T(128)S(1)}, u32[]{:S(2)}) copy-start(f32[4]{0:T(128)S(1)} %compare_convert_fusion) | copy-start | bytes 52
  69.6 6.1 copy-start.12
  69.6 47.8 %all-gather.37.cloned.1.call-start = ((), (), s32[]{:S(2)}) async-start(), calls=%async_computation.3 | async-start | bytes 1310720 | tf_op jit(solution)/shard_map/all_gather | solution.py:179
  71.0 6.6 copy-start.24
  71.0 7.2 copy-start.18
  71.1 10.8 copy-start.19
  71.5 4.1 collective-permute-start
  75.5 19.0 copy-start.25
  75.7 18.9 copy-start.22
  76.9 244.4 %all-gather.47.cloned.1.call-start = ((), (), s32[]{:S(2)}) async-start(), calls=%async_computation.8 | async-start | bytes 8912896 | tf_op jit(solution)/shard_map/all_gather | solution.py:25
  133.2 4.9 copy-start.44
  133.2 5.5 copy-start.36
  133.2 6.1 copy-start.37
  138.0 321.3 %reduce-scatter.7.cloned.1.call-start = ((), (), s32[]{:S(2)}) async-start(), calls=%async_computation.16 | async-start | bytes 2228224
  182.9 5.1 copy-start.26
  182.9 5.1 copy-start.33
  344.2 116.1 %copy-start.16 = (bf16[512,128]{1,0:T(8,128)(2,1)S(1)}, bf16[512,128]{1,0:T(8,128)(2,1)}, u32[]{:S(2)}) copy-start(bf16[512,128]{1,0:T(8,128)(2,1)} %param.20) | copy-start | bytes 393220
  344.3 168.1 %all-gather.41.cloned.1.call-start = ((), (), s32[]{:S(2)}) async-start(), calls=%async_computation.5 | async-start | bytes 2228224 | tf_op jit(solution)/shard_map/all_gather | solution.py:161
  461.1 79.9 %all-gather.45.cloned.1.call-start = ((), (), s32[]{:S(2)}) async-start(), calls=%async_computation.7 | async-start | bytes 1310720 | tf_op jit(solution)/shard_map/all_gather | solution.py:178
  516.4 10.2 copy-start
  516.4 7.0 copy-start.29
  516.4 7.0 copy-start.30
  516.4 7.0 copy-start.31
  516.4 7.0 copy-start.32
  517.9 7.7 copy-start.21
  517.9 47.8 %all-gather.43.cloned.1.call-start = ((), (), s32[]{:S(2)}) async-start(), calls=%async_computation.6 | async-start | bytes 1310720 | tf_op jit(solution)/shard_map/all_gather | solution.py:179
  518.6 3.8 collective-permute-start.1
  525.3 242.6 %all-gather.49.cloned.1.call-start = ((), (), s32[]{:S(2)}) async-start(), calls=%async_computation.9 | async-start | bytes 8912896 | tf_op jit(solution)/shard_map/all_gather | solution.py:25
  580.6 4.5 copy-start.20
  584.5 451.8 %all-gather.55.cloned.1.call-start = ((), (), s32[]{:S(2)}) async-start(), calls=%async_computation.12 | async-start | bytes 8912896 | tf_op jit(solution)/shard_map/all_gather | solution.py:44
  594.9 547.6 %all-gather.53.cloned.1.call-start = ((), (), s32[]{:S(2)}) async-start(), calls=%async_computation.11 | async-start | bytes 8912896 | tf_op jit(solution)/shard_map/all_gather | solution.py:44
  600.5 727.5 %all-gather.51.cloned.1.call-start = ((), (), s32[]{:S(2)}) async-start(), calls=%async_computation.10 | async-start | bytes 8912896 | tf_op jit(solution)/shard_map/all_gather | solution.py:44
  605.1 806.3 %reduce-scatter.9.cloned.1.call-start = ((), (), s32[]{:S(2)}) async-start(), calls=%async_computation.17 | async-start | bytes 2228224
  642.0 4.2 copy-start.8
  642.0 4.2 copy-start.11
  642.0 4.2 copy-start.27
  768.0 11.8 copy-start.1
  768.0 11.8 copy-start.39
  768.0 11.8 copy-start.40
  789.2 805.7 %all-gather.61.cloned.1.call-start = ((), (), s32[]{:S(2)}) async-start(), calls=%async_computation.15 | async-start | bytes 8912896 | tf_op jit(solution)/shard_map/all_gather | solution.py:44
  792.3 988.2 %all-gather.57.cloned.1.call-start = ((), (), s32[]{:S(2)}) async-start(), calls=%async_computation.13 | async-start | bytes 8912896 | tf_op jit(solution)/shard_map/all_gather | solution.py:44
  794.8 1170.6 %all-gather.59.cloned.1.call-start = ((), (), s32[]{:S(2)}) async-start(), calls=%async_computation.14 | async-start | bytes 8912896 | tf_op jit(solution)/shard_map/all_gather | solution.py:44
  796.1 2.7 copy-start.13
  796.2 142.6 %copy-start.14 = (bf16[512,256]{1,0:T(8,128)(2,1)S(1)}, bf16[512,256]{1,0:T(8,128)(2,1)}, u32[]{:S(2)}) copy-start(bf16[512,256]{1,0:T(8,128)(2,1)} %convolution_convert_fusion.4) | copy-start | bytes 786436
  796.2 239.3 %copy-start.43 = (s32[2]{0:T(128)S(1)}, s32[2]{0:T(128)}, u32[]{:S(2)}) copy-start(s32[2]{0:T(128)} %param.35) | copy-start | bytes 28
  1332.8 79.6 %copy-start.15 = (bf16[512,128]{1,0:T(8,128)(2,1)S(1)}, bf16[512,128]{1,0:T(8,128)(2,1)}, u32[]{:S(2)}) copy-start(bf16[512,128]{1,0:T(8,128)(2,1)} %add_convert_fusion.1) | copy-start | bytes 393220
  (15 other events, 27.4 us)
Sparse Core Ops, SparseCore 0:
  10.6 53.4 all-gather.34
  69.7 22.9 all-gather.38
  94.5 22.8 all-gather.36
  138.1 183.1 all-gather.46
  344.4 114.8 reduce-scatter.6
  462.4 49.9 all-gather.40
  518.0 22.8 all-gather.44
  542.8 22.8 all-gather.42
  584.6 183.1 all-gather.48
  769.5 186.3 all-gather.54
  957.7 184.7 all-gather.52
  1144.1 183.7 all-gather.50
  1332.1 79.2 reduce-scatter.8
  1413.0 181.7 all-gather.60
  1597.1 183.2 all-gather.56
  1782.1 183.2 all-gather.58
